TPU v7x, 32 devices: a whole 2x2x4 slice. The times are simulated.
32 devices in a mesh: row: 4 (over z), col: 8 (over y, x, core).
Axes of the slice: x: 2, y: 2, z: 4, core: 2. Of those that a mesh axis runs over, the one named last changes fastest.
Arguments:
- factor: float32 [4, 1024, 4096], P(None, 'row', 'col'), may hold values from -0.125 to 0.125
- panel_inverse: float32 [4, 1024, 1024], P(None, 'row', 'col')
- sim_maps: float32 [4, 1024, 128], P(None, 'row'), may hold values from -6 to 6
- harmonics: bfloat16 [28000, 4096], P('col', 'row'), may hold values from -0.09375 to 0.09375
Outputs:
- solved: float32 [4, 1024, 128], P(None, 'row')
- projected: float32 [128, 28000], P('row', 'col')
All inputs are finite; a program needn't handle non-finite values.
Results may differ from a plain program's by a relative error of at most 0.0029.
Values sent between devices are 32-bit elements; how exact they have to be, the bound alone decides.
A program may use at most 64 MiB of HBM per device.

v0:
```python
import functools

import jax
import jax.numpy as jnp
from jax import lax
from jax.experimental import pallas as pl
from jax.experimental.pallas import tpu as pltpu
from jax.sharding import PartitionSpec as P

MESH = pl.DeviceIdType.MESH
CHUNK = 512
LANES = 128
SUBLANES = 8


def split(value):
    high = value.astype(jnp.bfloat16)
    low = (value - high.astype(jnp.float32)).astype(jnp.bfloat16)
    return high, low


def dot3(mat_high, mat_low, value):
    high, low = split(value)
    mul = functools.partial(jnp.dot, preferred_element_type=jnp.float32)
    return mul(mat_high, high) + (mul(mat_high, low) + mul(mat_low, high))


def kernel(
    n_row, n_col, factor_hbm, inv_hbm, sim_hbm, harm_hbm, solved_ref, proj_ref,
    factor, inv, sim, harm, f_high, f_low, i_high, i_low,
    partial, gathered, piece, xbuf, xint, sol, stacked, outs, landed,
    load_sem, rs_send, rs_recv, bc_send, bc_recv, ag_send, ag_recv, pj_send, pj_recv,
):
    panels, rows, maps = sim.shape
    cols = inv.shape[2]
    part = rows // n_col
    out_rows = maps // n_row
    stages = 2 * panels - 1
    modes = harm.shape[0]
    chunks = outs.shape[0]
    r, c = lax.axis_index("row"), lax.axis_index("col")
    me = r * n_col + c
    total = n_row * n_col

    loads = [
        pltpu.make_async_copy(src, dst, load_sem.at[i])
        for i, (src, dst) in enumerate(
            ((sim_hbm, sim), (inv_hbm, inv), (factor_hbm, factor), (harm_hbm, harm))
        )
    ]
    for load in loads:
        load.start()

    barrier = pltpu.get_barrier_semaphore()

    def greet(d, carry):
        peer = (me + d) % total
        pl.semaphore_signal(
            barrier, inc=1, device_id=(peer // n_col, peer % n_col), device_id_type=MESH
        )
        return carry

    lax.fori_loop(1, total, greet, 0)
    xint[...] = jnp.zeros_like(xint)
    loads[0].wait()
    loads[1].wait()
    for k in range(panels):
        i_high[k], i_low[k] = split(inv[k])
    pl.semaphore_wait(barrier, total - 1)

    mine = pl.ds(pl.multiple_of(c * part, part), part)
    owner = (r * rows + c * part) // cols
    inside = (r * rows + c * part) % cols
    place = pl.ds(pl.multiple_of(inside, part), part)
    pieces = cols // part

    def spread(stage, source):
        def one(d, carry):
            pltpu.make_async_remote_copy(
                src_ref=source,
                dst_ref=xbuf.at[stage, place],
                send_sem=bc_send.at[stage],
                recv_sem=bc_recv.at[stage],
                device_id=((r + d) % n_row, owner),
                device_id_type=MESH,
            ).start()
            return carry

        @pl.when(owner != c)
        def _():
            one(0, 0)

        @pl.when(owner == c)
        def _():
            xbuf[stage, place] = source[...]

        lax.fori_loop(1, n_row, one, 0)

    def drain(sem, ref):
        pltpu.make_async_copy(ref, ref, sem).wait()

    def take(stage):
        @pl.when(owner != c)
        def _():
            drain(bc_recv.at[stage], xbuf.at[stage])

        @pl.when(owner == c)
        def _():
            drain(bc_recv.at[stage], xbuf.at[stage, pl.ds(0, (pieces - 1) * part)])

    def reduce(stage, value):
        partial[stage] = value

        def one(d, carry):
            peer = (c + d) % n_col
            pltpu.make_async_remote_copy(
                src_ref=partial.at[stage, pl.ds(pl.multiple_of(peer * part, part), part)],
                dst_ref=gathered.at[stage, d - 1],
                send_sem=rs_send.at[stage],
                recv_sem=rs_recv.at[stage],
                device_id=(r, peer),
                device_id_type=MESH,
            ).start()
            return carry

        lax.fori_loop(1, n_col, one, 0)
        return

    def reduced(stage):
        drain(rs_recv.at[stage], gathered.at[stage])
        total_value = partial[stage, mine]
        for d in range(n_col - 1):
            total_value = total_value + gathered[stage, d]
        return total_value

    spread(0, sim.at[0, mine])
    for stage in range(stages):
        take(stage)
        if stage % 2 == 0:
            k = stage // 2
            reduce(stage, dot3(i_high[k], i_low[k], xbuf[stage]))
            if stage == 0:
                loads[2].wait()
                for j in range(1, panels):
                    f_high[j - 1], f_low[j - 1] = split(factor[j])
            piece[stage] = reduced(stage)
            if stage + 1 < stages:
                spread(stage + 1, piece.at[stage])

            def share(d, carry):
                peer = (c + d) % n_col
                pltpu.make_async_remote_copy(
                    src_ref=piece.at[stage],
                    dst_ref=sol.at[k, mine],
                    send_sem=ag_send.at[k],
                    recv_sem=ag_recv.at[k],
                    device_id=(r, peer),
                    device_id_type=MESH,
                ).start()
                return carry

            lax.fori_loop(1, n_col, share, 0)
            sol[k, mine] = piece[stage]
        else:
            k = (stage + 1) // 2
            xint[pl.ds(k - 1, cols, stride=panels), :] = xbuf[stage]
            reduce(stage, dot3(f_high[k - 1], f_low[k - 1], xint[...]))
            piece[stage] = sim[k, mine] - reduced(stage)
            spread(stage + 1, piece.at[stage])

    rest = pl.ds(0, rows - part)
    loads[3].wait()
    for k in range(panels):
        drain(ag_recv.at[k], sol.at[k, rest])
        value = sol[k]
        solved_ref[k] = value
        stacked[pl.ds(k, rows, stride=panels), :] = value
    turned = jnp.transpose(stacked[...], (1, 0)).astype(jnp.bfloat16)
    for i in range(chunks):
        size = min(CHUNK, modes - i * CHUNK)
        outs[i, :, :size] = lax.dot_general(
            turned, harm[i * CHUNK : i * CHUNK + size, :],
            (((1,), (1,)), ((), ())), preferred_element_type=jnp.float32,
        )

        def send(d, carry):
            peer = (r + d) % n_row
            pltpu.make_async_remote_copy(
                src_ref=outs.at[i, pl.ds(pl.multiple_of(peer * out_rows, out_rows), out_rows)],
                dst_ref=landed.at[i, d - 1],
                send_sem=pj_send.at[i],
                recv_sem=pj_recv.at[i],
                device_id=(peer, c),
                device_id_type=MESH,
            ).start()
            return carry

        lax.fori_loop(1, n_row, send, 0)

    own = pl.ds(pl.multiple_of(r * out_rows, out_rows), out_rows)
    for i in range(chunks):
        size = min(CHUNK, modes - i * CHUNK)
        drain(pj_recv.at[i], landed.at[i])
        value = outs[i, own]
        for d in range(n_row - 1):
            value = value + landed[i, d]
        proj_ref[:, i * CHUNK : i * CHUNK + size] = value[:, :size]

    for stage in range(stages):
        drain(rs_send.at[stage], gathered.at[stage])

        @pl.when(owner != c)
        def _():
            drain(bc_send.at[stage], sol.at[0, pl.ds(0, n_row * part)])

        @pl.when(owner == c)
        def _():
            drain(bc_send.at[stage], sol.at[0, pl.ds(0, (n_row - 1) * part)])

    for k in range(panels):
        drain(ag_send.at[k], sol.at[k, rest])
    for i in range(chunks):
        drain(pj_send.at[i], landed.at[i])


def fused(n_row, n_col, factor, inv, sim, harm):
    panels, rows, maps = sim.shape
    cols = inv.shape[2]
    modes = harm.shape[0]
    part = rows // n_col
    stages = 2 * panels - 1
    chunks = -(-modes // CHUNK)
    f32, bf16 = jnp.float32, jnp.bfloat16
    any_space = pl.BlockSpec(memory_space=pl.ANY)
    vmem = pl.BlockSpec(memory_space=pltpu.VMEM)
    dma = pltpu.SemaphoreType.DMA
    return pl.pallas_call(
        functools.partial(kernel, n_row, n_col),
        out_shape=(
            jax.ShapeDtypeStruct(sim.shape, f32),
            jax.ShapeDtypeStruct((maps // n_row, modes), f32),
        ),
        in_specs=[any_space] * 4,
        out_specs=(vmem, vmem),
        scratch_shapes=[
            pltpu.VMEM(factor.shape, f32),
            pltpu.VMEM(inv.shape, f32),
            pltpu.VMEM(sim.shape, f32),
            pltpu.VMEM(harm.shape, bf16),
            pltpu.VMEM((panels - 1,) + factor.shape[1:], bf16),
            pltpu.VMEM((panels - 1,) + factor.shape[1:], bf16),
            pltpu.VMEM(inv.shape, bf16),
            pltpu.VMEM(inv.shape, bf16),
            pltpu.VMEM((stages, rows, maps), f32),
            pltpu.VMEM((stages, n_col - 1, part, maps), f32),
            pltpu.VMEM((stages, part, maps), f32),
            pltpu.VMEM((stages, cols, maps), f32),
            pltpu.VMEM((cols * panels, maps), f32),
            pltpu.VMEM(sim.shape, f32),
            pltpu.VMEM((rows * panels, maps), f32),
            pltpu.VMEM((chunks, maps, CHUNK), f32),
            pltpu.VMEM((chunks, n_row - 1, maps // n_row, CHUNK), f32),
            dma((4,)),
            dma((stages,)), dma((stages,)), dma((stages,)), dma((stages,)),
            dma((panels,)), dma((panels,)),
            dma((chunks,)), dma((chunks,)),
        ],
        compiler_params=pltpu.CompilerParams(
            collective_id=0, has_side_effects=True, vmem_limit_bytes=48 * 1024 * 1024
        ),
    )(factor, inv, sim, harm)


def plain(factor, panel_inverse, sim_maps, harmonics):
    panels = factor.shape[0]
    row_count = factor.shape[1]
    col_count = factor.shape[2] // panels
    map_count = sim_maps.shape[2]
    col_index = lax.axis_index("col")
    columns = jnp.zeros((col_count, panels, map_count), jnp.float32)
    results = []
    for panel in range(panels):
        flat_cols = columns.reshape(col_count * panels, map_count)
        partial_value = jnp.dot(
            factor[panel], flat_cols,
            precision=lax.Precision.HIGHEST, preferred_element_type=jnp.float32,
        )
        update = lax.psum(partial_value, "col")
        rhs_now = sim_maps[panel] - update
        whole = lax.all_gather(rhs_now, "row", axis=0, tiled=True)
        piece = lax.dynamic_slice_in_dim(whole, col_index * col_count, col_count, 0)
        partial_inv = jnp.dot(
            panel_inverse[panel], piece,
            precision=lax.Precision.HIGHEST, preferred_element_type=jnp.float32,
        )
        result = lax.psum(partial_inv, "col")
        whole_solved = lax.all_gather(result, "row", axis=0, tiled=True)
        solved_piece = lax.dynamic_slice_in_dim(whole_solved, col_index * col_count, col_count, 0)
        columns = columns.at[:, panel, :].set(solved_piece)
        results.append(result)
    solved = jnp.stack(results)
    solved_low = solved.astype(jnp.bfloat16)
    stacked = jnp.transpose(solved_low, (1, 0, 2)).reshape(row_count * panels, map_count)
    projected = lax.psum_scatter(
        lax.dot_general(
            stacked, harmonics, (((0,), (1,)), ((), ())), preferred_element_type=jnp.float32
        ),
        "row", scatter_dimension=0, tiled=True,
    )
    return (solved, projected)


def solution(mesh):
    n_row, n_col = mesh.shape["row"], mesh.shape["col"]

    def local(factor, panel_inverse, sim_maps, harmonics):
        _, rows, maps = sim_maps.shape
        cols = panel_inverse.shape[2]
        part = rows // n_col
        fits = (
            rows % n_col == 0
            and part % SUBLANES == 0
            and cols % part == 0
            and cols % LANES == 0
            and maps % LANES == 0
            and maps // n_row % SUBLANES == 0
            and rows % cols == 0
        )
        if not fits:
            return plain(factor, panel_inverse, sim_maps, harmonics)
        return fused(n_row, n_col, factor, panel_inverse, sim_maps, harmonics)

    in_specs = (P(None, "row", "col"), P(None, "row", "col"), P(None, "row", None), P("col", "row"))
    out_specs = (P(None, "row", None), P("row", "col"))
    return jax.shard_map(local, mesh=mesh, in_specs=in_specs, out_specs=out_specs, check_vma=False)
```

profile of v0, /device:TPU:0, one launch (start us, length us, event | category | flops | bytes accessed | tf_op | source)
XLA Modules:
  0.0 112.0 jit_solution(727378125246462350)
XLA Ops:
  0.6 0.0 copy-start
  0.6 1.6 %copy-done = f32[4,256,512]{2,1,0:T(8,128)S(1)} copy-done((f32[4,256,512]{2,1,0:T(8,128)S(1)}, f32[4,256,512]{2,1,0:T(8,128)}, u32[]{:S(2)}) %copy-start) | copy-done | bytes 2097176
  2.2 0.0 copy-start.1
  2.2 1.0 copy-done.1
  3.3 0.0 copy-start.2
  3.3 1.0 copy-done.2
  4.3 106.1 %shard_map.59 = (f32[4,256,128]{2,1,0:T(8,128)S(1)}, f32[32,3500]{1,0:T(8,128)S(1)}) custom-call(f32[4,256,512]{2,1,0:T(8,128)S(1)} %copy-done, f32[4,256,128]{2,1,0:T(8,128)S(1)} %copy-done.1, f32[4,256,128]{2,1,0:T(8,128)S(1)} %copy-done.2, bf16[3500,1024]{1,0:T(8,128)(2,1)} %harm_hbm.1), custom_call_target="tpu_custom_call" | custom-call | tf_op jit(solution)/shard_map/pallas_call | solution.py:237
  110.5 0.8 copy.8
  111.3 0.8 copy.9
Async XLA Ops:
  0.6 1.6 %copy-start = (f32[4,256,512]{2,1,0:T(8,128)S(1)}, f32[4,256,512]{2,1,0:T(8,128)}, u32[]{:S(2)}) copy-start(f32[4,256,512]{2,1,0:T(8,128)} %factor_hbm.1) | copy-start | bytes 6291460
  2.2 1.0 copy-start.1
  3.3 1.0 copy-start.2
where the time goes:
time: 112 us
  Pallas kernels  106 us (95%)
  local copies, waits for them, and re-layouts  5.23 us (5%)
    pallas_call x1, Pallas kernels, fused(): pl.pallas_call(functools.partial(kernel, n_row, n_col), out_shape=(jax.Sh...  106 us
    unnamed x8, local copies, waits for them, and re-layouts  5.23 us

commit v1 on v0

v1 whole, which is shorter than its diff:
```python
import functools

import jax
import jax.numpy as jnp
from jax import lax
from jax.experimental import pallas as pl
from jax.experimental.pallas import tpu as pltpu
from jax.sharding import PartitionSpec as P

MESH = pl.DeviceIdType.MESH
CHUNK = 512
LANES = 128
SUBLANES = 8
F32, BF16 = jnp.float32, jnp.bfloat16


def split(value):
    high = value.astype(BF16)
    low = (value - high.astype(F32)).astype(BF16)
    return high, low


def mul(left, right):
    return jnp.dot(left, right, preferred_element_type=F32)


def mul_nt(left, right):
    return lax.dot_general(left, right, (((1,), (1,)), ((), ())), preferred_element_type=F32)


def flip(index, bits):
    step = 1
    while step <= bits:
        if bits & step:
            index = index + (1 - 2 * ((index // step) % 2)) * step
        step *= 2
    return index


def spread_rows(shape, stride, offset):
    row = lax.broadcasted_iota(jnp.int32, shape, 0)
    col = lax.broadcasted_iota(jnp.int32, shape, 1)
    return jnp.where(col == row * stride + offset, 1.0, 0.0).astype(BF16)


def drain(sem, ref):
    pltpu.make_async_copy(ref, ref, sem).wait()


def kernel(
    n_row, n_col, factor_hbm, inv_hbm, sim_hbm, harm_hbm, solved_ref, proj_ref,
    factor, inv, sim, harm, mats, mats_high, mats_low, off_high, off_low, given, turn,
    acts, sol, across, part, landed, place, turned, outs, relayed, final,
    load_sem, ag_send, ag_recv, g_send, g_recv, p_send, p_recv, so_send, so_recv,
    xa_send, xa_recv, rs_send, rs_recv, pj_send, rl_recv, fi_recv,
):
    panels, rows, maps = sim.shape
    cols = inv.shape[2]
    own = maps // n_col
    out_rows = maps // n_row
    stages = 2 * panels - 1
    modes = harm.shape[0]
    chunks = outs.shape[0]
    wide = rows * n_row
    r, c = lax.axis_index("row"), lax.axis_index("col")

    def remote(source, target, send, recv, row, col):
        pltpu.make_async_remote_copy(
            src_ref=source, dst_ref=target, send_sem=send, recv_sem=recv,
            device_id=(row, col), device_id_type=MESH,
        ).start()

    loads = [pltpu.make_async_copy(sim_hbm, sim, load_sem.at[0])]
    loads.append(pltpu.make_async_copy(inv_hbm, inv, load_sem.at[1]))
    for k in range(1, panels):
        loads.append(pltpu.make_async_copy(factor_hbm.at[k], factor.at[k - 1], load_sem.at[1 + k]))
    loads.append(pltpu.make_async_copy(harm_hbm, harm, load_sem.at[1 + panels]))
    for load in loads:
        load.start()

    barrier = pltpu.get_barrier_semaphore()

    def greet_row(d, carry):
        pl.semaphore_signal(
            barrier, inc=1, device_id=((r + d) % n_row, c), device_id_type=MESH
        )
        return carry

    def greet_col(d, carry):
        pl.semaphore_signal(
            barrier, inc=1, device_id=(r, (c + d) % n_col), device_id_type=MESH
        )
        return carry

    lax.fori_loop(1, n_row, greet_row, 0)
    lax.fori_loop(1, n_col, greet_col, 0)

    my_maps = pl.ds(pl.multiple_of(c * own, own), own)
    my_rows = pl.ds(pl.multiple_of(r * rows, rows), rows)
    my_cols = pl.ds(pl.multiple_of(c * cols, cols), cols)

    loads[0].wait()
    for k in range(panels):
        turn[...] = jnp.transpose(sim[k], (1, 0))
        given[k] = turn[my_maps, :]
    acts[0, :, my_rows] = given[0]
    loads[1].wait()
    same = spread_rows((cols, cols), 1, 0)
    for k in range(panels):
        high, low = split(inv[k])
        mats[2 * k, my_cols, :] = mul_nt(same, high) + mul_nt(same, low)
    for k in range(1, panels):
        loads[1 + k].wait()
        high, low = split(factor[k - 1])
        for j in range(k):
            pick = spread_rows((cols, cols * panels), panels, j)
            first, second = mul_nt(pick, high), mul_nt(pick, low)
            if j == k - 1:
                mats[2 * k - 1, my_cols, :] = first + second
            else:
                at = (k - j - 2) * rows
                off_high[j, :, at : at + rows] = first.astype(BF16)
                off_low[j, :, at : at + rows] = second.astype(BF16)
    for k in range(panels):
        place[k] = spread_rows((rows, rows * panels), panels, k)
    pl.semaphore_wait(barrier, n_row + n_col - 2)

    def to_rows(t):
        def one(d, carry):
            remote(acts.at[t, :, my_rows], acts.at[t, :, my_rows],
                   ag_send.at[t], ag_recv.at[t, r], (r + d) % n_row, c)
            return carry

        lax.fori_loop(1, n_row, one, 0)

    def gather(n):
        block = mats.at[n, my_cols]
        for d in range(2, n_col, 2):
            remote(block, block, g_send.at[n], g_recv.at[n, d // 2 - 1], r, flip(c, d))
        remote(block, block, p_send.at[n], p_recv.at[n], r, flip(c, 1))

    def complete(n):
        for d in range(2, n_col, 2):
            block = mats.at[n, pl.ds(pl.multiple_of(flip(c, d) * cols, cols), cols)]
            drain(g_recv.at[n, d // 2 - 1], block)
            remote(block, block, p_send.at[n], p_recv.at[n], r, flip(c, 1))
        drain(p_recv.at[n], mats.at[n, pl.ds(0, n_col // 2 * cols)])
        mats_high[n], mats_low[n] = split(mats[n])

    half = r // (n_row // 2)
    near = r + half * (n_row - 1 - 2 * r)

    def apply(t):
        total = jnp.zeros((2 * own, rows), F32)
        total_low = jnp.zeros((own, rows), F32)
        for i in range(n_row):
            if i == 0:
                source = r
            else:
                source = (i - 1) + jnp.where(i - 1 >= near, 1, 0)
                source = source + half * (n_row - 1 - 2 * source)
            there = pl.ds(pl.multiple_of(source * rows, rows), rows)
            if i > 0:
                drain(ag_recv.at[t, source], acts.at[t, :, there])
            high, low = split(acts[t, :, there])
            both = jnp.concatenate([high, low], axis=0)
            total = total + mul(both, mats_high[t, there, :])
            total_low = total_low + mul(high, mats_low[t, there, :])
        return total[:own] + (total[own:] + total_low)

    def width(j):
        return (panels - 2 - j) * rows

    to_rows(0)
    gather(0)
    gather(1)
    complete(0)
    for t in range(stages):
        value = apply(t)
        if t % 2 == 0:
            k = t // 2
            if t + 1 < stages:
                acts[t + 1, :, my_rows] = value
                to_rows(t + 1)
            sol[k, my_maps, :] = value

            def share(d, carry):
                remote(sol.at[k, my_maps], sol.at[k, my_maps],
                       so_send.at[k], so_recv.at[k], r, (c + d) % n_col)
                return carry

            lax.fori_loop(1, n_col, share, 0)
            j = k - 1
            if 0 <= j < panels - 2:
                drain(xa_recv.at[j], across.at[j, pl.ds(0, (n_col - 1) * own)])
                high, low = split(across[j])
                w = width(j)
                part[j, :, :w] = mul(high, off_high[j, :, :w]) + (
                    mul(high, off_low[j, :, :w]) + mul(low, off_high[j, :, :w])
                )

                def reduce(d, carry):
                    peer = (c + d) % n_col
                    remote(
                        part.at[j, pl.ds(pl.multiple_of(peer * own, own), own), pl.ds(0, w)],
                        landed.at[j, d - 1, :, pl.ds(0, w)],
                        rs_send.at[j], rs_recv.at[j], r, peer,
                    )
                    return carry

                lax.fori_loop(1, n_col, reduce, 0)
        else:
            k = (t + 1) // 2
            for j in range(k - 1):
                at = (k - j - 2) * rows
                if at == 0:
                    drain(rs_recv.at[j], landed.at[j, :, :, pl.ds(0, width(j))])
                value = value + part[j, my_maps, at : at + rows]
                for d in range(n_col - 1):
                    value = value + landed[j, d, :, at : at + rows]
            acts[t + 1, :, my_rows] = given[k] - value
            to_rows(t + 1)
            j = k - 1
            if j < panels - 2:
                def turn_over(d, carry):
                    peer = (c + d) % n_col
                    remote(
                        acts.at[t, :, pl.ds(pl.multiple_of(peer * cols, cols), cols)],
                        across.at[j, my_maps],
                        xa_send.at[j], xa_recv.at[j], r, peer,
                    )
                    return carry

                lax.fori_loop(1, n_col, turn_over, 0)
                across[j, my_maps, :] = acts[t, :, my_cols]
        if t + 2 < stages:
            gather(t + 2)
        if t % 2 == 1:
            k = t // 2
            drain(so_recv.at[k], sol.at[k, pl.ds(0, (n_col - 1) * own)])
            solved_ref[k] = jnp.transpose(sol[k], (1, 0))
            spread = mul(sol[k].astype(BF16), place[k])
            turned[...] = spread if k == 0 else turned[...] + spread
        if t + 1 < stages:
            complete(t + 1)

    loads[-1].wait()
    last = panels - 1
    drain(so_recv.at[last], sol.at[last, pl.ds(0, (n_col - 1) * own)])
    maps_now = (turned[...] + mul(sol[last].astype(BF16), place[last])).astype(BF16)

    partner = flip(r, 1)
    odd = r % 2 == 1

    def slab(s):
        return pl.ds(pl.multiple_of(s * out_rows, out_rows), out_rows)

    def relays(s):
        return (s // 2 != r // 2) & ((s > r) == odd)

    def passes(s):
        return (s // 2 != r // 2) & ((s > r) != odd)

    for i in range(chunks):
        size = min(CHUNK, modes - i * CHUNK)
        outs[i, :, :size] = mul_nt(maps_now, harm[i * CHUNK : i * CHUNK + size, :])
        for s in range(n_row):
            @pl.when(passes(s))
            def _():
                remote(outs.at[i, slab(s)], relayed.at[i, s],
                       pj_send.at[i], rl_recv.at[i, s], partner, c)
    for i in range(chunks):
        remote(outs.at[i, slab(partner)], final.at[i, 0],
               pj_send.at[i], fi_recv.at[i], partner, c)
    solved_ref[last] = jnp.transpose(sol[last], (1, 0))
    for i in range(chunks):
        for s in range(n_row):
            @pl.when(relays(s))
            def _():
                drain(rl_recv.at[i, s], relayed.at[i, s])
                outs[i, slab(s)] = outs[i, slab(s)] + relayed[i, s]
                pair = r // 2
                slot = pair + jnp.where(pair < s // 2, 1, 0)
                remote(outs.at[i, slab(s)], final.at[i, slot],
                       pj_send.at[i], fi_recv.at[i], s, c)
    for i in range(chunks):
        size = min(CHUNK, modes - i * CHUNK)
        drain(fi_recv.at[i], final.at[i])
        value = outs[i, slab(r)]
        for d in range(n_row // 2):
            value = value + final[i, d]
        proj_ref[:, i * CHUNK : i * CHUNK + size] = value[:, :size]

    for t in range(stages):
        drain(ag_send.at[t], acts.at[t, :, pl.ds(0, (n_row - 1) * rows)])
        drain(g_send.at[t], mats.at[t, pl.ds(0, (n_col // 2 - 1) * cols)])
        drain(p_send.at[t], mats.at[t, pl.ds(0, n_col // 2 * cols)])
    for k in range(panels):
        drain(so_send.at[k], sol.at[k, pl.ds(0, (n_col - 1) * own)])
    for j in range(panels - 2):
        drain(xa_send.at[j], across.at[j, pl.ds(0, (n_col - 1) * own)])
        drain(rs_send.at[j], landed.at[j, :, :, pl.ds(0, width(j))])
    for i in range(chunks):
        drain(pj_send.at[i], outs.at[i, pl.ds(0, (n_row - 1) * out_rows)])


def fused(n_row, n_col, factor, inv, sim, harm):
    panels, rows, maps = sim.shape
    cols = inv.shape[2]
    modes = harm.shape[0]
    own = maps // n_col
    wide = rows * n_row
    out_rows = maps // n_row
    stages = 2 * panels - 1
    chunks = -(-modes // CHUNK)
    off_width = (panels - 2) * rows
    any_space = pl.BlockSpec(memory_space=pl.ANY)
    vmem = pl.BlockSpec(memory_space=pltpu.VMEM)
    dma = pltpu.SemaphoreType.DMA
    return pl.pallas_call(
        functools.partial(kernel, n_row, n_col),
        out_shape=(
            jax.ShapeDtypeStruct(sim.shape, F32),
            jax.ShapeDtypeStruct((out_rows, modes), F32),
        ),
        in_specs=[any_space] * 4,
        out_specs=(vmem, vmem),
        scratch_shapes=[
            pltpu.VMEM((panels - 1,) + factor.shape[1:], F32),
            pltpu.VMEM(inv.shape, F32),
            pltpu.VMEM(sim.shape, F32),
            pltpu.VMEM(harm.shape, BF16),
            pltpu.VMEM((stages, wide, rows), F32),
            pltpu.VMEM((stages, wide, rows), BF16),
            pltpu.VMEM((stages, wide, rows), BF16),
            pltpu.VMEM((panels - 2, cols, off_width), BF16),
            pltpu.VMEM((panels - 2, cols, off_width), BF16),
            pltpu.VMEM((panels, own, rows), F32),
            pltpu.VMEM((maps, rows), F32),
            pltpu.VMEM((stages, own, wide), F32),
            pltpu.VMEM((panels, maps, rows), F32),
            pltpu.VMEM((panels - 2, maps, cols), F32),
            pltpu.VMEM((panels - 2, maps, off_width), F32),
            pltpu.VMEM((panels - 2, n_col - 1, own, off_width), F32),
            pltpu.VMEM((panels, rows, rows * panels), BF16),
            pltpu.VMEM((maps, rows * panels), F32),
            pltpu.VMEM((chunks, maps, CHUNK), F32),
            pltpu.VMEM((chunks, n_row, out_rows, CHUNK), F32),
            pltpu.VMEM((chunks, n_row // 2, out_rows, CHUNK), F32),
            dma((panels + 2,)),
            dma((stages,)), dma((stages, n_row)),
            dma((stages,)), dma((stages, n_col // 2 - 1)),
            dma((stages,)), dma((stages,)),
            dma((panels,)), dma((panels,)),
            dma((panels - 2,)), dma((panels - 2,)),
            dma((panels - 2,)), dma((panels - 2,)),
            dma((chunks,)), dma((chunks, n_row)), dma((chunks,)),
        ],
        compiler_params=pltpu.CompilerParams(
            collective_id=0, has_side_effects=True, vmem_limit_bytes=56 * 1024 * 1024
        ),
    )(factor, inv, sim, harm)


def plain(factor, panel_inverse, sim_maps, harmonics):
    panels = factor.shape[0]
    row_count = factor.shape[1]
    col_count = factor.shape[2] // panels
    map_count = sim_maps.shape[2]
    col_index = lax.axis_index("col")
    columns = jnp.zeros((col_count, panels, map_count), jnp.float32)
    results = []
    for panel in range(panels):
        flat_cols = columns.reshape(col_count * panels, map_count)
        partial_value = jnp.dot(
            factor[panel], flat_cols,
            precision=lax.Precision.HIGHEST, preferred_element_type=jnp.float32,
        )
        update = lax.psum(partial_value, "col")
        rhs_now = sim_maps[panel] - update
        whole = lax.all_gather(rhs_now, "row", axis=0, tiled=True)
        piece = lax.dynamic_slice_in_dim(whole, col_index * col_count, col_count, 0)
        partial_inv = jnp.dot(
            panel_inverse[panel], piece,
            precision=lax.Precision.HIGHEST, preferred_element_type=jnp.float32,
        )
        result = lax.psum(partial_inv, "col")
        whole_solved = lax.all_gather(result, "row", axis=0, tiled=True)
        solved_piece = lax.dynamic_slice_in_dim(whole_solved, col_index * col_count, col_count, 0)
        columns = columns.at[:, panel, :].set(solved_piece)
        results.append(result)
    solved = jnp.stack(results)
    solved_low = solved.astype(jnp.bfloat16)
    stacked = jnp.transpose(solved_low, (1, 0, 2)).reshape(row_count * panels, map_count)
    projected = lax.psum_scatter(
        lax.dot_general(
            stacked, harmonics, (((0,), (1,)), ((), ())), preferred_element_type=jnp.float32
        ),
        "row", scatter_dimension=0, tiled=True,
    )
    return (solved, projected)


def solution(mesh):
    n_row, n_col = mesh.shape["row"], mesh.shape["col"]

    def local(factor, panel_inverse, sim_maps, harmonics):
        panels, rows, maps = sim_maps.shape
        cols = panel_inverse.shape[2]
        fits = (
            panels > 2
            and n_row % 2 == 0
            and n_col > 2
            and n_col & (n_col - 1) == 0
            and rows * n_row == cols * n_col
            and rows % LANES == 0
            and cols % LANES == 0
            and maps % LANES == 0
            and maps % (n_col * SUBLANES) == 0
            and maps % (n_row * SUBLANES) == 0
        )
        if not fits:
            return plain(factor, panel_inverse, sim_maps, harmonics)
        return fused(n_row, n_col, factor, panel_inverse, sim_maps, harmonics)

    in_specs = (P(None, "row", "col"), P(None, "row", "col"), P(None, "row", None), P("col", "row"))
    out_specs = (P(None, "row", None), P("row", "col"))
    return jax.shard_map(local, mesh=mesh, in_specs=in_specs, out_specs=out_specs, check_vma=False)
```

time: 112 us -> 100 us (0.89)
  Pallas kernels: 106 us -> 95.2 us
  local copies, waits for them, and re-layouts: 5.23 us -> 3.68 us
    pallas_call x1, Pallas kernels: 106 us -> 95.2 us  [fused(): pl.pallas_call(functools.partial(kernel, n_row, n_col), out_shape=(jax.Sh...]
    unnamed x8 -> x2, local copies, waits for them, and re-layouts: 5.23 us -> 3.68 us
where the time goes in v1:
time: 100 us; the launch traced here: 99.5 us
  Pallas kernels  95.2 us (95%)
  local copies, waits for them, and re-layouts  3.68 us (4%)
    pallas_call x1, Pallas kernels, fused(): pl.pallas_call(functools.partial(kernel, n_row, n_col), out_shape=(jax.Sh...  95.2 us
    unnamed x2, local copies, waits for them, and re-layouts  3.68 us

profile of v1, /device:TPU:0, one launch (start us, length us, event | category | flops | bytes accessed | tf_op | source)
XLA Modules:
  0.0 99.5 jit_solution(9198263027348822939)
XLA Ops:
  0.6 95.2 %shard_map.59 = (f32[4,256,128]{2,1,0:T(8,128)}, f32[32,3500]{1,0:T(8,128)}) custom-call(f32[4,256,512]{2,1,0:T(8,128)} %factor_hbm.1, f32[4,256,128]{2,1,0:T(8,128)} %inv_hbm.1, f32[4,256,128]{2,1,0:T(8,128)} %sim_hbm.1, bf16[3500,1024]{1,0:T(8,128)(2,1)} %harm_hbm.1), custom_call_target="tpu_custom_call" | custom-call | tf_op jit(solution)/shard_map/pallas_call | solution.py:320
  95.9 1.9 %copy.8 = f32[4,256,128]{2,1,0:T(8,128)} copy(f32[4,256,128]{2,1,0:T(8,128)} %get-tuple-element.4) | data formatting | bytes 1048576
  97.7 1.8 %copy.9 = f32[32,3500]{1,0:T(8,128)} copy(f32[32,3500]{1,0:T(8,128)} %get-tuple-element.5) | data formatting | bytes 896000

commit v2 on v1

--- a/solution.py
+++ b/solution.py
@@ -51,7 +51,7 @@
     n_row, n_col, factor_hbm, inv_hbm, sim_hbm, harm_hbm, solved_ref, proj_ref,
     factor, inv, sim, harm, mats, mats_high, mats_low, off_high, off_low, given, turn,
     acts, sol, across, part, landed, place, turned, outs, relayed, final,
-    load_sem, ag_send, ag_recv, g_send, g_recv, p_send, p_recv, so_send, so_recv,
+    load_sem, ag_send, ag_recv, g_send, g_recv, d_recv, p_send, p_recv, so_send, so_recv,
     xa_send, xa_recv, rs_send, rs_recv, pj_send, rl_recv, fi_recv,
 ):
     panels, rows, maps = sim.shape
@@ -118,9 +118,9 @@
             if j == k - 1:
                 mats[2 * k - 1, my_cols, :] = first + second
             else:
-                at = (k - j - 2) * rows
-                off_high[j, :, at : at + rows] = first.astype(BF16)
-                off_low[j, :, at : at + rows] = second.astype(BF16)
+                at = pl.ds(j * cols, cols)
+                off_high[k - 2, at, :] = first.astype(BF16)
+                off_low[k - 2, at, :] = second.astype(BF16)
     for k in range(panels):
         place[k] = spread_rows((rows, rows * panels), panels, k)
     pl.semaphore_wait(barrier, n_row + n_col - 2)
@@ -133,17 +133,37 @@
 
         lax.fori_loop(1, n_row, one, 0)
 
-    def gather(n):
+    def piece(n, peer):
+        return mats.at[n, pl.ds(pl.multiple_of(peer * cols, cols), cols)]
+
+    def to_partner(n, block):
+        remote(block, block, p_send.at[n], p_recv.at[n], r, flip(c, 1))
+
+    def issue(n):
         block = mats.at[n, my_cols]
-        for d in range(2, n_col, 2):
-            remote(block, block, g_send.at[n], g_recv.at[n, d // 2 - 1], r, flip(c, d))
-        remote(block, block, p_send.at[n], p_recv.at[n], r, flip(c, 1))
-
-    def complete(n):
-        for d in range(2, n_col, 2):
-            block = mats.at[n, pl.ds(pl.multiple_of(flip(c, d) * cols, cols), cols)]
-            drain(g_recv.at[n, d // 2 - 1], block)
-            remote(block, block, p_send.at[n], p_recv.at[n], r, flip(c, 1))
+        for i in range(2):
+            remote(block, block, g_send.at[n], g_recv.at[n, i], r, flip(c, 2 + 2 * i))
+        if n == 0:
+            remote(block, block, g_send.at[n], d_recv.at[n], r, flip(c, 6))
+        to_partner(n, block)
+
+    def relay(n):
+        for i in range(2):
+            peer = flip(c, 2 + 2 * i)
+            block = piece(n, peer)
+            drain(g_recv.at[n, i], block)
+            if n > 0:
+                at = peer * cols + i * (cols // 2)
+                some = mats.at[n, pl.ds(pl.multiple_of(at, cols // 2), cols // 2)]
+                remote(some, some, g_send.at[n], d_recv.at[n], r, flip(c, 4 - 2 * i))
+            to_partner(n, block)
+
+    def finish(n):
+        block = piece(n, flip(c, 6))
+        drain(d_recv.at[n], block)
+        to_partner(n, block)
+
+    def land(n):
         drain(p_recv.at[n], mats.at[n, pl.ds(0, n_col // 2 * cols)])
         mats_high[n], mats_low[n] = split(mats[n])
 
@@ -168,13 +188,20 @@
             total_low = total_low + mul(high, mats_low[t, there, :])
         return total[:own] + (total[own:] + total_low)
 
-    def width(j):
-        return (panels - 2 - j) * rows
+    def share(k):
+        def one(d, carry):
+            remote(sol.at[k, my_maps], sol.at[k, my_maps],
+                   so_send.at[k], so_recv.at[k], r, (c + d) % n_col)
+            return carry
+
+        lax.fori_loop(1, n_col, one, 0)
 
     to_rows(0)
-    gather(0)
-    gather(1)
-    complete(0)
+    for n in range(3):
+        issue(n)
+    relay(0)
+    finish(0)
+    land(0)
     for t in range(stages):
         value = apply(t)
         if t % 2 == 0:
@@ -184,40 +211,34 @@
                 to_rows(t + 1)
             sol[k, my_maps, :] = value
 
-            def share(d, carry):
-                remote(sol.at[k, my_maps], sol.at[k, my_maps],
-                       so_send.at[k], so_recv.at[k], r, (c + d) % n_col)
-                return carry
-
-            lax.fori_loop(1, n_col, share, 0)
             j = k - 1
             if 0 <= j < panels - 2:
                 drain(xa_recv.at[j], across.at[j, pl.ds(0, (n_col - 1) * own)])
-                high, low = split(across[j])
-                w = width(j)
-                part[j, :, :w] = mul(high, off_high[j, :, :w]) + (
-                    mul(high, off_low[j, :, :w]) + mul(low, off_high[j, :, :w])
-                )
+                total = jnp.zeros((maps, rows), F32)
+                for i in range(j + 1):
+                    at = pl.ds(i * cols, cols)
+                    high, low = split(across[i])
+                    total = total + mul(high, off_high[j, at, :]) + (
+                        mul(high, off_low[j, at, :]) + mul(low, off_high[j, at, :])
+                    )
+                part[j] = total
 
                 def reduce(d, carry):
                     peer = (c + d) % n_col
                     remote(
-                        part.at[j, pl.ds(pl.multiple_of(peer * own, own), own), pl.ds(0, w)],
-                        landed.at[j, d - 1, :, pl.ds(0, w)],
-                        rs_send.at[j], rs_recv.at[j], r, peer,
+                        part.at[j, pl.ds(pl.multiple_of(peer * own, own), own)],
+                        landed.at[j, d - 1], rs_send.at[j], rs_recv.at[j], r, peer,
                     )
                     return carry
 
                 lax.fori_loop(1, n_col, reduce, 0)
         else:
             k = (t + 1) // 2
-            for j in range(k - 1):
-                at = (k - j - 2) * rows
-                if at == 0:
-                    drain(rs_recv.at[j], landed.at[j, :, :, pl.ds(0, width(j))])
-                value = value + part[j, my_maps, at : at + rows]
+            if k > 1:
+                drain(rs_recv.at[k - 2], landed.at[k - 2])
+                value = value + part[k - 2, my_maps, :]
                 for d in range(n_col - 1):
-                    value = value + landed[j, d, :, at : at + rows]
+                    value = value + landed[k - 2, d]
             acts[t + 1, :, my_rows] = given[k] - value
             to_rows(t + 1)
             j = k - 1
@@ -233,19 +254,29 @@
 
                 lax.fori_loop(1, n_col, turn_over, 0)
                 across[j, my_maps, :] = acts[t, :, my_cols]
+        if t == 0:
+            relay(1)
         if t + 2 < stages:
-            gather(t + 2)
-        if t % 2 == 1:
-            k = t // 2
-            drain(so_recv.at[k], sol.at[k, pl.ds(0, (n_col - 1) * own)])
-            solved_ref[k] = jnp.transpose(sol[k], (1, 0))
-            spread = mul(sol[k].astype(BF16), place[k])
-            turned[...] = spread if k == 0 else turned[...] + spread
+            relay(t + 2)
+        if t + 3 < stages:
+            issue(t + 3)
         if t + 1 < stages:
-            complete(t + 1)
+            finish(t + 1)
+        if t == stages - 2:
+            for k in range(panels - 1):
+                share(k)
+        if t == stages - 1:
+            share(panels - 1)
+        if t + 1 < stages:
+            land(t + 1)
 
     loads[-1].wait()
     last = panels - 1
+    for k in range(last):
+        drain(so_recv.at[k], sol.at[k, pl.ds(0, (n_col - 1) * own)])
+        solved_ref[k] = jnp.transpose(sol[k], (1, 0))
+        spread = mul(sol[k].astype(BF16), place[k])
+        turned[...] = spread if k == 0 else turned[...] + spread
     drain(so_recv.at[last], sol.at[last, pl.ds(0, (n_col - 1) * own)])
     maps_now = (turned[...] + mul(sol[last].astype(BF16), place[last])).astype(BF16)
 
@@ -299,7 +330,7 @@
         drain(so_send.at[k], sol.at[k, pl.ds(0, (n_col - 1) * own)])
     for j in range(panels - 2):
         drain(xa_send.at[j], across.at[j, pl.ds(0, (n_col - 1) * own)])
-        drain(rs_send.at[j], landed.at[j, :, :, pl.ds(0, width(j))])
+        drain(rs_send.at[j], landed.at[j])
     for i in range(chunks):
         drain(pj_send.at[i], outs.at[i, pl.ds(0, (n_row - 1) * out_rows)])
 
@@ -313,8 +344,7 @@
     out_rows = maps // n_row
     stages = 2 * panels - 1
     chunks = -(-modes // CHUNK)
-    off_width = (panels - 2) * rows
-    any_space = pl.BlockSpec(memory_space=pl.ANY)
+    any_space = pl.BlockSpec(memory_space=pltpu.HBM)
     vmem = pl.BlockSpec(memory_space=pltpu.VMEM)
     dma = pltpu.SemaphoreType.DMA
     return pl.pallas_call(
@@ -333,15 +363,15 @@
             pltpu.VMEM((stages, wide, rows), F32),
             pltpu.VMEM((stages, wide, rows), BF16),
             pltpu.VMEM((stages, wide, rows), BF16),
-            pltpu.VMEM((panels - 2, cols, off_width), BF16),
-            pltpu.VMEM((panels - 2, cols, off_width), BF16),
+            pltpu.VMEM((panels - 2, (panels - 2) * cols, rows), BF16),
+            pltpu.VMEM((panels - 2, (panels - 2) * cols, rows), BF16),
             pltpu.VMEM((panels, own, rows), F32),
             pltpu.VMEM((maps, rows), F32),
             pltpu.VMEM((stages, own, wide), F32),
             pltpu.VMEM((panels, maps, rows), F32),
             pltpu.VMEM((panels - 2, maps, cols), F32),
-            pltpu.VMEM((panels - 2, maps, off_width), F32),
-            pltpu.VMEM((panels - 2, n_col - 1, own, off_width), F32),
+            pltpu.VMEM((panels - 2, maps, rows), F32),
+            pltpu.VMEM((panels - 2, n_col - 1, own, rows), F32),
             pltpu.VMEM((panels, rows, rows * panels), BF16),
             pltpu.VMEM((maps, rows * panels), F32),
             pltpu.VMEM((chunks, maps, CHUNK), F32),
@@ -349,7 +379,7 @@
             pltpu.VMEM((chunks, n_row // 2, out_rows, CHUNK), F32),
             dma((panels + 2,)),
             dma((stages,)), dma((stages, n_row)),
-            dma((stages,)), dma((stages, n_col // 2 - 1)),
+            dma((stages,)), dma((stages, 2)), dma((stages,)),
             dma((stages,)), dma((stages,)),
             dma((panels,)), dma((panels,)),
             dma((panels - 2,)), dma((panels - 2,)),
@@ -357,7 +387,7 @@
             dma((chunks,)), dma((chunks, n_row)), dma((chunks,)),
         ],
         compiler_params=pltpu.CompilerParams(
-            collective_id=0, has_side_effects=True, vmem_limit_bytes=56 * 1024 * 1024
+            collective_id=0, has_side_effects=True, vmem_limit_bytes=53 * 1024 * 1024
         ),
     )(factor, inv, sim, harm)
 
@@ -410,8 +440,7 @@
         fits = (
             panels > 2
             and n_row % 2 == 0
-            and n_col > 2
-            and n_col & (n_col - 1) == 0
+            and n_col == 2 ** 3
             and rows * n_row == cols * n_col
             and rows % LANES == 0
             and cols % LANES == 0

time: 100 us -> 86.1 us (0.86)
  Pallas kernels: 95.2 us -> 83.4 us
  local copies, waits for them, and re-layouts: 3.68 us -> 1.56 us
    pallas_call x1, Pallas kernels: 95.2 us -> 83.4 us  [fused(): pl.pallas_call(functools.partial(kernel, n_row, n_col), out_shape=(jax.Sh...]
    unnamed x2, local copies, waits for them, and re-layouts: 3.68 us -> 1.56 us
where the time goes in v2:
time: 86.1 us; the launch traced here: 85.6 us
  Pallas kernels  83.4 us (97%)
  local copies, waits for them, and re-layouts  1.56 us (2%)
    pallas_call x1, Pallas kernels, fused(): pl.pallas_call(functools.partial(kernel, n_row, n_col), out_shape=(jax.Sh...  83.4 us

profile of v2, /device:TPU:0, one launch (start us, length us, event | category | flops | bytes accessed | tf_op | source)
XLA Modules:
  0.0 85.6 jit_solution(13671203843283560777)
XLA Ops:
  0.6 83.4 %shard_map.59 = (f32[4,256,128]{2,1,0:T(8,128)S(1)}, f32[32,3500]{1,0:T(8,128)S(1)}) custom-call(f32[4,256,512]{2,1,0:T(8,128)} %factor_hbm.1, f32[4,256,128]{2,1,0:T(8,128)} %inv_hbm.1, f32[4,256,128]{2,1,0:T(8,128)} %sim_hbm.1, bf16[3500,1024]{1,0:T(8,128)(2,1)} %harm_hbm.1), custom_call_target="tpu_custom_call" | custom-call | tf_op jit(solution)/shard_map/pallas_call | solution.py:350
  84.1 0.8 copy.8
  84.8 0.8 copy.9

commit v3 on v2

--- a/solution.py
+++ b/solution.py
@@ -50,8 +50,9 @@
 def kernel(
     n_row, n_col, factor_hbm, inv_hbm, sim_hbm, harm_hbm, solved_ref, proj_ref,
     factor, inv, sim, harm, mats, mats_high, mats_low, off_high, off_low, given, turn,
+    begin, first, first_high, first_low, first_part, first_landed,
     acts, sol, across, part, landed, place, turned, outs, relayed, final,
-    load_sem, ag_send, ag_recv, g_send, g_recv, d_recv, p_send, p_recv, so_send, so_recv,
+    load_sem, fs_send, fs_recv, fr_send, fr_recv, ag_send, ag_recv, g_send, g_recv, d_recv, p_send, p_recv, so_send, so_recv,
     xa_send, xa_recv, rs_send, rs_recv, pj_send, rl_recv, fi_recv,
 ):
     panels, rows, maps = sim.shape
@@ -92,38 +93,55 @@
         )
         return carry
 
+    pieces = rows // cols
+    origin = c // pieces
+
+    def greet_origin(peer, carry):
+        pl.semaphore_signal(barrier, inc=1, device_id=(origin, peer), device_id_type=MESH)
+        return carry
+
     lax.fori_loop(1, n_row, greet_row, 0)
     lax.fori_loop(1, n_col, greet_col, 0)
+
+    @pl.when(origin != r)
+    def _():
+        lax.fori_loop(0, n_col, greet_origin, 0)
+
 
     my_maps = pl.ds(pl.multiple_of(c * own, own), own)
     my_rows = pl.ds(pl.multiple_of(r * rows, rows), rows)
     my_cols = pl.ds(pl.multiple_of(c * cols, cols), cols)
 
     loads[0].wait()
-    for k in range(panels):
+    begin[...] = jnp.transpose(sim[0], (1, 0))
+    for k in range(1, panels):
         turn[...] = jnp.transpose(sim[k], (1, 0))
         given[k] = turn[my_maps, :]
-    acts[0, :, my_rows] = given[0]
     loads[1].wait()
     same = spread_rows((cols, cols), 1, 0)
     for k in range(panels):
         high, low = split(inv[k])
-        mats[2 * k, my_cols, :] = mul_nt(same, high) + mul_nt(same, low)
+        high, low = mul_nt(same, high), mul_nt(same, low)
+        if k == 0:
+            first_high[...] = high.astype(BF16)
+            first_low[...] = low.astype(BF16)
+        else:
+            mats[2 * k, my_cols, :] = high + low
     for k in range(1, panels):
         loads[1 + k].wait()
         high, low = split(factor[k - 1])
         for j in range(k):
             pick = spread_rows((cols, cols * panels), panels, j)
-            first, second = mul_nt(pick, high), mul_nt(pick, low)
+            top, rest = mul_nt(pick, high), mul_nt(pick, low)
             if j == k - 1:
-                mats[2 * k - 1, my_cols, :] = first + second
+                mats[2 * k - 1, my_cols, :] = top + rest
             else:
                 at = pl.ds(j * cols, cols)
-                off_high[k - 2, at, :] = first.astype(BF16)
-                off_low[k - 2, at, :] = second.astype(BF16)
+                off_high[k - 2, at, :] = top.astype(BF16)
+                off_low[k - 2, at, :] = rest.astype(BF16)
     for k in range(panels):
         place[k] = spread_rows((rows, rows * panels), panels, k)
-    pl.semaphore_wait(barrier, n_row + n_col - 2)
+    pl.semaphore_wait(barrier, n_row + n_col - 2 + (n_row - 1) * pieces)
 
     def to_rows(t):
         def one(d, carry):
@@ -143,8 +161,6 @@
         block = mats.at[n, my_cols]
         for i in range(2):
             remote(block, block, g_send.at[n], g_recv.at[n, i], r, flip(c, 2 + 2 * i))
-        if n == 0:
-            remote(block, block, g_send.at[n], d_recv.at[n], r, flip(c, 6))
         to_partner(n, block)
 
     def relay(n):
@@ -152,10 +168,9 @@
             peer = flip(c, 2 + 2 * i)
             block = piece(n, peer)
             drain(g_recv.at[n, i], block)
-            if n > 0:
-                at = peer * cols + i * (cols // 2)
-                some = mats.at[n, pl.ds(pl.multiple_of(at, cols // 2), cols // 2)]
-                remote(some, some, g_send.at[n], d_recv.at[n], r, flip(c, 4 - 2 * i))
+            at = peer * cols + i * (cols // 2)
+            some = mats.at[n, pl.ds(pl.multiple_of(at, cols // 2), cols // 2)]
+            remote(some, some, g_send.at[n], d_recv.at[n], r, flip(c, 4 - 2 * i))
             to_partner(n, block)
 
     def finish(n):
@@ -196,14 +211,49 @@
 
         lax.fori_loop(1, n_col, one, 0)
 
-    to_rows(0)
-    for n in range(3):
-        issue(n)
-    relay(0)
-    finish(0)
-    land(0)
+    def reduce(source, target, send, recv):
+        def one(d, carry):
+            peer = (c + d) % n_col
+            remote(source.at[pl.ds(pl.multiple_of(peer * own, own), own)],
+                   target.at[d - 1], send, recv, r, peer)
+            return carry
+
+        lax.fori_loop(1, n_col, one, 0)
+
+    def start_out(d, carry):
+        for i in range(pieces):
+            remote(begin.at[my_maps, pl.ds(i * cols, cols)], first.at[my_maps],
+                   fs_send, fs_recv, (r + d) % n_row, r * pieces + i)
+        return carry
+
+    lax.fori_loop(1, n_row, start_out, 0)
+    issue(1)
+    issue(2)
+
+    @pl.when(origin == r)
+    def _():
+        at = (c % pieces) * cols
+        first[...] = begin[:, pl.ds(pl.multiple_of(at, cols), cols)]
+
+    @pl.when(origin != r)
+    def _():
+        drain(fs_recv, first)
+
+    high, low = split(first[...])
+    first_part[...] = mul(high, first_high[...]) + (
+        mul(high, first_low[...]) + mul(low, first_high[...])
+    )
+    reduce(first_part, first_landed, fr_send, fr_recv)
+    relay(1)
+    issue(3)
     for t in range(stages):
-        value = apply(t)
+        if t == 0:
+            drain(fr_recv, first_landed)
+            value = first_part[my_maps, :]
+            for d in range(n_col - 1):
+                value = value + first_landed[d]
+        else:
+            value = apply(t)
         if t % 2 == 0:
             k = t // 2
             if t + 1 < stages:
@@ -223,15 +273,7 @@
                     )
                 part[j] = total
 
-                def reduce(d, carry):
-                    peer = (c + d) % n_col
-                    remote(
-                        part.at[j, pl.ds(pl.multiple_of(peer * own, own), own)],
-                        landed.at[j, d - 1], rs_send.at[j], rs_recv.at[j], r, peer,
-                    )
-                    return carry
-
-                lax.fori_loop(1, n_col, reduce, 0)
+                reduce(part.at[j], landed.at[j], rs_send.at[j], rs_recv.at[j])
         else:
             k = (t + 1) // 2
             if k > 1:
@@ -254,19 +296,17 @@
 
                 lax.fori_loop(1, n_col, turn_over, 0)
                 across[j, my_maps, :] = acts[t, :, my_cols]
-        if t == 0:
-            relay(1)
-        if t + 2 < stages:
-            relay(t + 2)
-        if t + 3 < stages:
-            issue(t + 3)
-        if t + 1 < stages:
-            finish(t + 1)
         if t == stages - 2:
             for k in range(panels - 1):
                 share(k)
         if t == stages - 1:
             share(panels - 1)
+        if t + 1 < stages:
+            finish(t + 1)
+        if t + 2 < stages:
+            relay(t + 2)
+        if t + 4 < stages:
+            issue(t + 4)
         if t + 1 < stages:
             land(t + 1)
 
@@ -322,7 +362,9 @@
             value = value + final[i, d]
         proj_ref[:, i * CHUNK : i * CHUNK + size] = value[:, :size]
 
-    for t in range(stages):
+    drain(fs_send, begin.at[pl.ds(0, (n_row - 1) * own)])
+    drain(fr_send, first_landed)
+    for t in range(1, stages):
         drain(ag_send.at[t], acts.at[t, :, pl.ds(0, (n_row - 1) * rows)])
         drain(g_send.at[t], mats.at[t, pl.ds(0, (n_col // 2 - 1) * cols)])
         drain(p_send.at[t], mats.at[t, pl.ds(0, n_col // 2 * cols)])
@@ -367,6 +409,12 @@
             pltpu.VMEM((panels - 2, (panels - 2) * cols, rows), BF16),
             pltpu.VMEM((panels, own, rows), F32),
             pltpu.VMEM((maps, rows), F32),
+            pltpu.VMEM((maps, rows), F32),
+            pltpu.VMEM((maps, cols), F32),
+            pltpu.VMEM((cols, rows), BF16),
+            pltpu.VMEM((cols, rows), BF16),
+            pltpu.VMEM((maps, rows), F32),
+            pltpu.VMEM((n_col - 1, own, rows), F32),
             pltpu.VMEM((stages, own, wide), F32),
             pltpu.VMEM((panels, maps, rows), F32),
             pltpu.VMEM((panels - 2, maps, cols), F32),
@@ -378,6 +426,7 @@
             pltpu.VMEM((chunks, n_row, out_rows, CHUNK), F32),
             pltpu.VMEM((chunks, n_row // 2, out_rows, CHUNK), F32),
             dma((panels + 2,)),
+            dma, dma, dma, dma,
             dma((stages,)), dma((stages, n_row)),
             dma((stages,)), dma((stages, 2)), dma((stages,)),
             dma((stages,)), dma((stages,)),
@@ -442,6 +491,7 @@
             and n_row % 2 == 0
             and n_col == 2 ** 3
             and rows * n_row == cols * n_col
+            and rows % cols == 0
             and rows % LANES == 0
             and cols % LANES == 0
             and maps % LANES == 0

time: 86.1 us -> 83.3 us (0.967)
  Pallas kernels: 83.4 us -> 80.9 us
    pallas_call x1, Pallas kernels: 83.4 us -> 80.9 us  [fused(): pl.pallas_call(functools.partial(kernel, n_row, n_col), out_shape=(jax.Sh...]
where the time goes in v3:
time: 83.3 us; the launch traced here: 83.1 us
  Pallas kernels  80.9 us (97%)
  local copies, waits for them, and re-layouts  1.56 us (2%)
    pallas_call x1, Pallas kernels, fused(): pl.pallas_call(functools.partial(kernel, n_row, n_col), out_shape=(jax.Sh...  80.9 us

profile of v3, /device:TPU:0, one launch (start us, length us, event | category | flops | bytes accessed | tf_op | source)
XLA Modules:
  0.0 83.1 jit_solution(14901060312855693966)
XLA Ops:
  0.6 80.9 %shard_map.59 = (f32[4,256,128]{2,1,0:T(8,128)S(1)}, f32[32,3500]{1,0:T(8,128)S(1)}) custom-call(f32[4,256,512]{2,1,0:T(8,128)} %factor_hbm.1, f32[4,256,128]{2,1,0:T(8,128)} %inv_hbm.1, f32[4,256,128]{2,1,0:T(8,128)} %sim_hbm.1, bf16[3500,1024]{1,0:T(8,128)(2,1)} %harm_hbm.1), custom_call_target="tpu_custom_call" | custom-call | tf_op jit(solution)/shard_map/pallas_call | solution.py:392
  81.5 0.8 copy.8
  82.3 0.8 copy.9
